TPU v7x, 32 devices: a whole 2x2x4 slice. The times are simulated.
32 devices in a mesh: narrow: 2 (over y), wide: 4 (over z), nys: 4 (over x, core).
Axes of the slice: x: 2, y: 2, z: 4, core: 2. Of those that a mesh axis runs over, the one named last changes fastest.
Arguments:
- centers: bfloat16 [32768, 1024], P(('narrow', 'wide', 'nys')), may hold values from -6 to 6
- weights: float32 [32768, 1000], P(('narrow', 'wide', 'nys')), may hold values from -6 to 6
- batch_points: bfloat16 [512, 1024], P(('narrow', 'wide', 'nys')), may hold values from -6 to 6
- labels: float32 [512, 1000], P(('narrow', 'wide', 'nys')), may hold values from -6 to 6
- nystrom_points: bfloat16 [2048, 1024], P(('narrow', 'nys')), may hold values from -6 to 6
- eigvecs: float32 [2048, 160], P(('narrow', 'nys')), may hold values from -0.125 to 0.125
- corrections: float32 [160], replicated, may hold values from 0.05 to 0.5
Outputs:
- new_weights: float32 [32768, 1000], P(('narrow', 'wide', 'nys'))
All inputs are finite; a program needn't handle non-finite values.
Results may differ from a plain program's by a relative error of at most 0.0003.
The roundings to bfloat16 on the way count: a program that leaves them out, or rounds other values in their place, can miss the bound.
Values may be sent and summed in bfloat16 or wider, within the bound.
No kernel may reach another device: no remote copies, remote signals or barrier semaphores. Data moves between devices by JAX's collectives and lax.ppermute only.
A program may use at most 64 MiB of HBM per device.

v0:
```python
import math

import jax
import jax.numpy as jnp
from jax import lax
from jax.sharding import PartitionSpec as P

BATCH = 512


RATE = 16.0
SPREAD = 4.0


def kernel_with(left, left_sq, right):
    cross = lax.dot_general(
        left, right, (((1,), (1,)), ((), ())), preferred_element_type=jnp.float32
    )
    right_sq = jnp.sum(jnp.square(right.astype(jnp.float32)), axis=1)
    dist = jnp.sqrt(jnp.maximum(left_sq[:, None] + right_sq[None, :] - 2.0 * cross, 0.0))
    radius = math.sqrt(2.0 * left.shape[1])
    return jnp.exp((radius - dist) / SPREAD).astype(jnp.bfloat16)


def squares(points):
    return jnp.sum(jnp.square(points.astype(jnp.float32)), axis=1)


def per_device(centers, weights, batch_points, labels, nystrom_points, eigvecs, corrections):
    batch_all = lax.all_gather(batch_points, ("narrow", "wide", "nys"), axis=0, tiled=True)
    points_all = lax.all_gather(nystrom_points, ("narrow", "nys"), axis=0, tiled=True)
    vectors_full = lax.all_gather(eigvecs, ("narrow", "nys"), axis=0, tiled=True)
    count = lax.axis_size(("narrow", "wide", "nys"))
    scale = (centers.shape[0] * count) ** (-0.5)
    center_sq = squares(centers)
    k_batch = kernel_with(centers, center_sq, batch_all)
    partial_value = (
        lax.dot_general(
            k_batch,
            weights.astype(jnp.bfloat16),
            (((0,), (0,)), ((), ())),
            preferred_element_type=jnp.float32,
        )
        * scale
    )
    rows = labels.shape[0]
    offset = lax.axis_index(("narrow", "wide", "nys")) * rows
    placed = lax.dynamic_update_slice(jnp.zeros_like(partial_value), labels, (offset, jnp.int32(0)))
    residual = lax.psum(partial_value - placed, ("narrow", "wide", "nys")).astype(jnp.bfloat16)
    k_nystrom = kernel_with(nystrom_points, squares(nystrom_points), batch_all)
    pulled = jnp.dot(k_nystrom, residual, preferred_element_type=jnp.float32)
    local_proj = lax.dot_general(
        eigvecs, pulled, (((0,), (0,)), ((), ())), precision=lax.Precision.HIGHEST
    )
    projected = lax.psum(local_proj, ("narrow", "nys"))
    scaled_proj = corrections[:, None] * projected
    gradient = jnp.dot(k_batch, residual, preferred_element_type=jnp.float32)
    corrected_all = jnp.dot(vectors_full, scaled_proj, precision=lax.Precision.HIGHEST).astype(
        jnp.bfloat16
    )
    tile_all = kernel_with(centers, center_sq, points_all)
    nystrom_term = jnp.dot(tile_all, corrected_all, preferred_element_type=jnp.float32)
    return weights - RATE / BATCH * (gradient - nystrom_term)


def solution(mesh):
    placed = (
        P(("narrow", "wide", "nys"), None),
        P(("narrow", "wide", "nys"), None),
        P(("narrow", "wide", "nys"), None),
        P(("narrow", "wide", "nys"), None),
        P(("narrow", "nys"), None),
        P(("narrow", "nys"), None),
        P(),
    )
    return jax.shard_map(
        per_device,
        mesh=mesh,
        in_specs=placed,
        out_specs=P(("narrow", "wide", "nys"), None),
        check_vma=False,
    )
```

profile of v0, /device:TPU:0, one launch (start us, length us, event | category | flops | bytes accessed | tf_op | source)
XLA Modules:
  0.0 260.3 jit_solution(16899667897856393778)
XLA Ops:
  6.5 0.0 all-gather.4.cloned.1.call-start
  6.5 0.7 all-gather.4.cloned.1.call-update
  7.3 0.0 all-gather.8.cloned.1.call-start
  7.3 0.7 all-gather.8.cloned.1.call-update
  8.0 0.0 all-reduce.3.cloned.1.call-start
  8.1 1.2 multiply_reduce_fusion.3
  9.3 2.1 multiply_reduce_fusion.1
  11.4 1.0 copy.8
  12.4 0.2 broadcast_in_dim.2
  12.7 5.5 %dynamic_update_slice.3 = f32[512,1000]{0,1:T(8,128)S(1)} dynamic-update-slice(f32[512,1000]{0,1:T(8,128)S(1)} %broadcast_in_dim.2, f32[16,1000]{0,1:T(8,128)S(1)} %copy.8, s32[]{:T(128)S(6)} %select_n.3, s32[]{:T(128)} %constant.9.clone.1) | dynamic-update-slice | bytes 128004 | tf_op jit(solution)/shard_map/dynamic_update_slice | solution.py:48
  18.2 48.4 %all-gather.4.cloned.1.call-done = bf16[512,1024]{1,0:T(8,128)(2,1)} async-done(((bf16[16,1024]{1,0:T(8,128)(2,1)}), bf16[512,1024]{1,0:T(8,128)(2,1)}) %all-gather.4.cloned.1.call-update) | async-done | bytes 1048592 | tf_op jit(solution)/shard_map/all_gather | solution.py:30
  66.6 1.5 multiply_reduce_fusion.2
  68.1 4.1 %exponential_convert_fusion.1 = bf16[1024,512]{1,0:T(8,128)(2,1)S(1)} fusion(bf16[1024,1024]{1,0:T(8,128)(2,1)} %param.7, bf16[512,1024]{1,0:T(8,128)(2,1)} %all-gather.4.cloned.1.call-done, f32[512]{0:T(512)S(1)} %multiply_reduce_fusion.2, f32[1024]{0:T(1024)S(1)} %multiply_reduce_fusion.1), kind=kOutput, calls=%fused_computation.6 | convolution fusion | flops 1077411840 | bytes 4200448 | tf_op jit(solution)/shard_map/dot_general | solution.py:16
  72.2 0.0 copy-done
  72.2 2.6 multiply_subtract_fusion.1
  74.8 61.8 %all-reduce.4 = bf16[512,1000]{0,1:T(8,128)(2,1)S(1)} all-reduce(f32[512,1000]{0,1:T(8,128)} %multiply_subtract_fusion.1), channel_id=1, replica_groups=mesh['narrow'=2,'wide'=4,'nys'=4] {'narrow','wide','nys'}, use_global_device_ids=true, to_apply=%region_2.0 | all-reduce | flops 512000 | bytes 3072000 | tf_op jit(solution)/shard_map/psum | solution.py:49
  136.6 0.0 copy-start.5
  136.6 2.4 fusion.13
  139.0 1.6 convolution_bitcast_fusion
  140.7 0.0 all-reduce.3.cloned.1.call-update
  140.7 0.2 all-gather.6.cloned.1.call-start
  140.9 0.3 all-gather.6.cloned.1.call-update
  141.3 0.0 all-gather.8.cloned.1.call-done
  141.3 53.8 %all-reduce.3.cloned.1.call-done = f32[160,1000]{1,0:T(8,128)} async-done(((f32[160,1000]{1,0:T(8,128)}), f32[160,1000]{1,0:T(8,128)}) %all-reduce.3.cloned.1.call-update) | async-done | bytes 640016 | tf_op jit(solution)/shard_map/psum | solution.py:55
  195.1 9.7 %fusion.14 = bf16[1000,2048]{1,0:T(8,128)(2,1)} fusion(f32[2048,160]{0,1:T(8,128)} %all-gather.8.cloned.1.call-done, f32[160,1000]{1,0:T(8,128)} %all-reduce.3.cloned.1.call-done, f32[160]{0:T(256)S(1)} %copy-done.5), kind=kOutput, calls=%fused_computation.22 | convolution fusion | flops 3932320000 | bytes 6047360 | tf_op jit(solution)/shard_map/dot_general | solution.py:58
  204.8 28.0 %all-gather.6.cloned.1.call-done = bf16[2048,1024]{1,0:T(8,128)(2,1)} async-done(((bf16[256,1024]{1,0:T(8,128)(2,1)}), bf16[2048,1024]{1,0:T(8,128)(2,1)}) %all-gather.6.cloned.1.call-update) | async-done | bytes 4194320 | tf_op jit(solution)/shard_map/all_gather | solution.py:31
  232.8 3.2 %multiply_reduce_fusion = f32[2048]{0:T(1024)S(1)} fusion(bf16[2048,1024]{1,0:T(8,128)(2,1)} %all-gather.6.cloned.1.call-done), kind=kLoop, calls=%fused_computation.1 | loop fusion | flops 6289408 | bytes 4202496 | tf_op jit(solution)/shard_map/reduce_sum | solution.py:19
  236.0 0.2 copy-done.3
  236.2 9.7 %exponential_convert_fusion = bf16[1024,2048]{1,0:T(8,128)(2,1)S(1)} fusion(bf16[1024,1024]{1,0:T(8,128)(2,1)} %param.7, bf16[2048,1024]{1,0:T(8,128)(2,1)S(1)} %copy-done.3, f32[2048]{0:T(1024)S(1)} %multiply_reduce_fusion, f32[1024]{0:T(1024)S(1)} %multiply_reduce_fusion.1), kind=kOutput, calls=%fused_computation | convolution fusion | flops 4309647360 | bytes 10498048 | tf_op jit(solution)/shard_map/dot_general | solution.py:16
  246.0 0.0 copy-start.1
  246.0 4.4 %fusion.30 = f32[1024,1000]{0,1:T(8,128)S(1)} fusion(bf16[1024,2048]{1,0:T(8,128)(2,1)S(1)} %exponential_convert_fusion, bf16[1000,2048]{1,0:T(8,128)(2,1)S(1)} %copy-done.2), kind=kOutput, calls=%fused_computation.38 | convolution fusion | flops 4194304000 | bytes 12386304 | tf_op jit(solution)/shard_map/dot_general | solution.py:62
  250.4 3.3 %multiply_subtract_fusion = f32[1024,1000]{0,1:T(8,128)} fusion(f32[1024,1000]{0,1:T(8,128)S(1)} %copy-done.1, f32[1024,1000]{0,1:T(8,128)S(1)} %fusion.30, bf16[1024,512]{1,0:T(8,128)(2,1)S(1)} %exponential_convert_fusion.1, bf16[512,1000]{0,1:T(8,128)(2,1)S(1)} %all-reduce.4), kind=kOutput, calls=%fused_computation.3 | convolution fusion | flops 1051648000 | bytes 14360576 | tf_op jit(solution)/shard_map/dot_general | solution.py:57
  (8 shorter events, 0.0 us)
Async XLA Ops:
  6.5 60.0 %all-gather.4.cloned.1.call-start = ((), (), s32[]{:S(2)}) async-start(), calls=%async_computation | async-start | bytes 1081344 | tf_op jit(solution)/shard_map/all_gather | solution.py:30
  7.3 134.0 %all-gather.8.cloned.1.call-start = ((), (), s32[]{:S(2)}) async-start(), calls=%async_computation.3 | async-start | bytes 1474560 | tf_op jit(solution)/shard_map/all_gather | solution.py:32
  8.0 187.1 %all-reduce.3.cloned.1.call-start = ((), (), s32[]{:S(2)}) async-start(), calls=%async_computation.2 | async-start | bytes 1310720 | tf_op jit(solution)/shard_map/psum | solution.py:55
  68.1 4.1 %copy-start = (f32[1024,1000]{0,1:T(8,128)S(1)}, f32[1024,1000]{0,1:T(8,128)}, u32[]{:S(2)}) copy-start(f32[1024,1000]{0,1:T(8,128)} %param.8) | copy-start | bytes 12288004
  74.8 64.3 %copy-start.4 = (f32[256,160]{0,1:T(8,128)S(1)}, f32[256,160]{0,1:T(8,128)}, u32[]{:S(2)}) copy-start(f32[256,160]{0,1:T(8,128)} %param.12) | copy-start | bytes 491524
  136.6 58.5 %copy-start.5 = (f32[160]{0:T(256)S(1)}, f32[160]{0:T(256)}, u32[]{:S(2)}) copy-start(f32[160]{0:T(256)} %param.13) | copy-start | bytes 1924
  140.7 92.1 %all-gather.6.cloned.1.call-start = ((), (), s32[]{:S(2)}) async-start(), calls=%async_computation.1 | async-start | bytes 4718592 | tf_op jit(solution)/shard_map/all_gather | solution.py:31
  232.8 3.4 %copy-start.3 = (bf16[2048,1024]{1,0:T(8,128)(2,1)S(1)}, bf16[2048,1024]{1,0:T(8,128)(2,1)}, u32[]{:S(2)}) copy-start(bf16[2048,1024]{1,0:T(8,128)(2,1)} %all-gather.6.cloned.1.call-done) | copy-start | bytes 12582916
  236.2 9.8 %copy-start.2 = (bf16[1000,2048]{1,0:T(8,128)(2,1)S(1)}, bf16[1000,2048]{1,0:T(8,128)(2,1)}, u32[]{:S(2)}) copy-start(bf16[1000,2048]{1,0:T(8,128)(2,1)} %fusion.14) | copy-start | bytes 12288004
  246.0 4.5 %copy-start.1 = (f32[1024,1000]{0,1:T(8,128)S(1)}, f32[1024,1000]{0,1:T(8,128)}, u32[]{:S(2)}) copy-start(f32[1024,1000]{0,1:T(8,128)} %param.8) | copy-start | bytes 12288004
Sparse Core Ops, SparseCore 0:
  10.2 56.3 all-gather.3
  68.4 26.0 all-gather.7
  140.8 54.1 all-reduce.2
  196.8 35.9 all-gather.5
where the time goes:
time: 261 us; the launch traced here: 260 us
  waiting for transfers between devices  132 us (51%)
  blocking collectives  61.8 us (24%)
  matrix products  37.9 us (15%)
  between operations  13.3 us (5%)
  other arithmetic  8.02 us (3%)
  local copies, waits for them, and re-layouts  7.05 us (3%)
    psum x1, blocking collectives, per_device(): lax.psum(partial_value - placed, ('narrow', 'wide', 'nys'))  61.8 us
    psum x1, waiting for transfers between devices, per_device(): projected = lax.psum(local_proj, ('narrow', 'nys'))  53.8 us
    all_gather x1, waiting for transfers between devices, per_device(): lax.all_gather(batch_points, ('narrow', 'wide', 'nys'), axis=0, tiled=True)  48.4 us
    all_gather x1, waiting for transfers between devices, per_device(): lax.all_gather(nystrom_points, ('narrow', 'nys'), axis=0, tiled=True)  28 us
    dot_general x2, matrix products, kernel_with(): lax.dot_general(left, right, (((1,), (1,)), ((), ())), preferred_element_...  13.8 us
    dot_general x1, matrix products, per_device(): jnp.dot(vectors_full, scaled_proj, precision=lax.Precision.HIGHEST)  9.72 us
    dynamic_update_slice x1, local copies, waits for them, and re-layouts, per_device(): lax.dynamic_update_slice(jnp.zeros_like(partial_value), labels, (offset,...  5.52 us
  transfers between devices with their start and end apart: 4, of which 3 were waited for; matrix products, arithmetic and copies ran while one was open for 12% of the time, Pallas kernels for 0%

commit v1 on v0

v1 whole, which is shorter than its diff:
```python
import functools
import itertools
import math

import jax
import jax.numpy as jnp
from jax import lax
from jax.experimental import pallas as pl
from jax.experimental.pallas import tpu as pltpu
from jax.sharding import PartitionSpec as P


RATE = 16.0
SPREAD = 4.0
AXES = ("narrow", "wide", "nys")
MIB = 1 << 20


def row_squares(points):
    return jnp.sum(jnp.square(points.astype(jnp.float32)), axis=1, keepdims=True)


def turned_row(column):
    return jnp.broadcast_to(column, (column.shape[0], 128)).T[:1]


def kernel_tile(left, right, right_sq):
    cross = lax.dot_general(
        left, right, (((1,), (1,)), ((), ())), preferred_element_type=jnp.float32
    )
    left_sq = row_squares(left)
    dist = jnp.sqrt(jnp.maximum(left_sq + right_sq - 2.0 * cross, 0.0))
    radius = math.sqrt(2.0 * left.shape[1])
    return jnp.exp((radius - dist) / SPREAD).astype(jnp.bfloat16)


def split3(value):
    high = value.astype(jnp.bfloat16)
    rest = value - high.astype(jnp.float32)
    mid = rest.astype(jnp.bfloat16)
    low = (rest - mid.astype(jnp.float32)).astype(jnp.bfloat16)
    return high, mid, low


def call(body, outs, *args, flops=0, exps=0, limit=None):
    size = lambda a: math.prod(a.shape) * a.dtype.itemsize
    moved = sum(map(size, args)) + sum(map(size, outs))
    single = len(outs) == 1
    vmem = pl.BlockSpec(memory_space=pltpu.VMEM)
    return pl.pallas_call(
        body,
        out_shape=outs[0] if single else tuple(outs),
        in_specs=[vmem] * len(args),
        out_specs=vmem if single else tuple([vmem] * len(outs)),
        compiler_params=pltpu.CompilerParams(vmem_limit_bytes=limit or moved + 2 * MIB),
        cost_estimate=pl.CostEstimate(
            flops=flops, bytes_accessed=moved, transcendentals=exps
        ),
    )(*args)


def shape(dims, dtype=jnp.float32):
    return jax.ShapeDtypeStruct(tuple(dims), dtype)


def join_body(*refs):
    out, start = refs[-1], 0
    for ref in refs[:-1]:
        out[start : start + ref.shape[0]] = ref[...]
        start += ref.shape[0]


def join(pieces):
    if len(pieces) == 1:
        return pieces[0]
    rows = sum(p.shape[0] for p in pieces)
    out = shape((rows,) + pieces[0].shape[1:], pieces[0].dtype)
    return call(join_body, [out], *pieces)


def sum_body(count, *refs):
    start = 0
    for out in refs[count:]:
        rows = out.shape[0]
        total = refs[0][start : start + rows]
        for ref in refs[1:count]:
            total = total + ref[start : start + rows]
        out[...] = total
        start += rows


def residual_body(scale, count, *refs):
    total = refs[0][...]
    for ref in refs[1:count]:
        total = total + ref[...]
    labels, out = refs[count:]
    outs = labels.shape[1]
    out[...] = jnp.zeros_like(out)
    out[:, :outs] = (total[:, :outs] * scale - labels[...]).astype(jnp.bfloat16)


def prep_body(weights, centers, corrections, weights_low, centers_sq, factors):
    outs = weights.shape[0]
    weights_low[:outs] = weights[...].astype(jnp.bfloat16)
    if weights_low.shape[0] > outs:
        weights_low[outs:] = jnp.zeros_like(weights_low[outs:])
    centers_sq[...] = turned_row(row_squares(centers[...]))
    q = corrections.shape[1]
    factors[...] = jnp.broadcast_to(corrections[...], (128, q)).T


def tile_body(start, kept, valued, *refs):
    refs = list(refs)
    points, centers, centers_sq = refs[:3]
    weights = refs[3] if valued else None
    scratch, sem = refs[-2:]
    tail = refs[-2 - (1 + kept + valued) : -2]
    tile = kernel_tile(points[...], centers[...], centers_sq[...])
    scratch[...] = tile
    copy = pltpu.make_async_copy(
        scratch, tail[0].at[pl.ds(start, points.shape[0])], sem
    )
    copy.start()
    if kept:
        tail[1][...] = tile
    if valued:
        tail[-1][...] = lax.dot_general(
            tile, weights[...], (((1,), (1,)), ((), ())), preferred_element_type=jnp.float32
        )
    copy.wait()


def tile_call(points, centers, centers_sq, buffer, start, total, kept=False, weights=None):
    n, features = points.shape
    n_centers = centers.shape[0]
    vmem = pl.BlockSpec(memory_space=pltpu.VMEM)
    hbm = pl.BlockSpec(memory_space=pl.ANY)
    args = [points, centers, centers_sq]
    specs = [vmem] * 3
    outs = [shape((total, n_centers), jnp.bfloat16)]
    flops = 2 * n * n_centers * features
    if kept:
        outs.append(shape((n, n_centers), jnp.bfloat16))
    if weights is not None:
        args.append(weights)
        specs.append(vmem)
        outs.append(shape((n, weights.shape[0])))
        flops += 2 * n * n_centers * weights.shape[0]
    alias = {}
    if buffer is not None:
        alias = {len(args): 0}
        args.append(buffer)
        specs.append(hbm)
    got = pl.pallas_call(
        functools.partial(tile_body, start, kept, weights is not None),
        out_shape=tuple(outs),
        in_specs=specs,
        out_specs=tuple([hbm] + [vmem] * (len(outs) - 1)),
        scratch_shapes=[pltpu.VMEM((n, n_centers), jnp.bfloat16), pltpu.SemaphoreType.DMA],
        input_output_aliases=alias,
        compiler_params=pltpu.CompilerParams(vmem_limit_bytes=9 * MIB),
        cost_estimate=pl.CostEstimate(
            flops=flops, bytes_accessed=4 * MIB, transcendentals=2 * n * n_centers
        ),
        name="tile",
    )(*args)
    return got if len(got) > 1 else got[0]


def value_body(tile, weights, value):
    value[...] = lax.dot_general(
        tile[...], weights[...], (((1,), (1,)), ((), ())), preferred_element_type=jnp.float32
    )


def pull_body(halves, count, last, *refs):
    refs = list(refs)
    batch, refs = refs[:halves], refs[halves:]
    points, vectors = refs[:count], refs[count : 2 * count]
    before = refs[2 * count] if last else None
    batch_sq = [turned_row(row_squares(b[...])) for b in batch]
    out, stack, tiles, parts = refs[-4:]
    q = vectors[0].shape[0]
    rows = batch[0].shape[0]
    start = 0
    for p, v in zip(points, vectors):
        n = p.shape[0]
        for k, part in enumerate(split3(v[...])):
            parts[k * q : (k + 1) * q, start : start + n] = part
        for k, i in enumerate((2, 1, 0, 1, 0, 0)):
            stack[k * q : (k + 1) * q, start : start + n] = parts[
                i * q : (i + 1) * q, start : start + n
            ]
        for h in range(halves):
            tiles[start : start + n, h * rows : (h + 1) * rows] = kernel_tile(
                p[...], batch[h][...], batch_sq[h]
            )
        start += n
    total = jnp.dot(parts[...], tiles[...], preferred_element_type=jnp.float32)
    total = total[2 * q :] + total[q : 2 * q] + total[:q]
    if before is not None:
        total = total + before[...]
    if out.dtype == jnp.bfloat16:
        for k, part in enumerate(split3(total)):
            out[k * q : (k + 1) * q] = part
    else:
        out[...] = total


def update_body(rate, halves, groups, *refs):
    refs = list(refs)
    residuals, pulling, factors = refs[:halves], refs[halves], refs[halves + 1]
    stacks = refs[halves + 2 : halves + 2 + groups]
    buffer, weights = refs[halves + 2 + groups : halves + 4 + groups]
    out, stack_v, buffer_v, weights_v, mixed, turned, sems, out_sems = refs[halves + 4 + groups :]
    outs, _ = weights.shape
    q = factors.shape[0]
    rows = residuals[0].shape[0]
    batch = halves * rows
    wide = stacks[0].shape[1]
    copies = [
        pltpu.make_async_copy(s, stack_v.at[:, pl.ds(i * wide, wide)], sems.at[i])
        for i, s in enumerate(stacks)
    ]
    copies.append(pltpu.make_async_copy(buffer, buffer_v, sems.at[groups]))
    copies.append(pltpu.make_async_copy(weights, weights_v, sems.at[groups + 1]))
    for copy in copies:
        copy.start()

    projected = None
    for h, r in enumerate(residuals):
        term = jnp.dot(
            pulling[:, h * rows : (h + 1) * rows], r[...], preferred_element_type=jnp.float32
        )
        projected = term if projected is None else projected + term
        turned[:, h * rows : (h + 1) * rows] = r[...].T
    projected = projected[2 * q :] + projected[q : 2 * q] + projected[:q]
    parts = split3(factors[:, :1] * projected)
    for k, i in enumerate((0, 1, 2, 0, 1, 0)):
        mixed[k * q : (k + 1) * q] = parts[i]

    for i in range(groups):
        copies[i].wait()
        corrected = lax.dot_general(
            mixed[...],
            stack_v[:, i * wide : (i + 1) * wide],
            (((0,), (0,)), ((), ())),
            preferred_element_type=jnp.float32,
        )
        turned[:, batch + i * wide : batch + (i + 1) * wide] = (-corrected).astype(jnp.bfloat16)
    copies[groups].wait()
    copies[groups + 1].wait()
    block = 256
    stores = []
    for i, start in enumerate(range(0, outs, block)):
        n = min(block, outs - start)
        total = jnp.dot(
            turned[start : start + n], buffer_v[...], preferred_element_type=jnp.float32
        )
        weights_v[start : start + n] = weights_v[start : start + n] - rate * total
        store = pltpu.make_async_copy(
            weights_v.at[pl.ds(start, n)], out.at[pl.ds(start, n)], out_sems.at[i]
        )
        store.start()
        stores.append(store)
    for store in stores:
        store.wait()


class Digits:
    def __init__(self, mesh):
        narrow, wide, nys = (mesh.shape[a] for a in AXES)
        pair = 2 if nys % 2 == 0 else 1
        self.sizes = (narrow, wide, nys // pair, pair)

    def perm(self, offsets):
        pairs = []
        for target in itertools.product(*(range(s) for s in self.sizes)):
            source = [(t + o) % s for t, o, s in zip(target, offsets, self.sizes)]
            pairs.append((self.flat(source), self.flat(target)))
        return pairs

    def flat(self, digits):
        index = 0
        for d, s in zip(digits, self.sizes):
            index = index * s + d
        return index

    def steps(self, dims):
        ranges = [range(s) if i in dims else (0,) for i, s in enumerate(self.sizes)]
        return list(itertools.product(*ranges))

    def fetch(self, value, offsets):
        if not any(offsets):
            return value
        return lax.ppermute(value, AXES, self.perm(offsets))

    def gather(self, value, dims):
        return [self.fetch(value, step) for step in self.steps(dims)]

    def scatter(self, pieces, dims):
        out = []
        for piece, step in zip(pieces, self.steps(dims)):
            back = tuple((s - o) % s for o, s in zip(step, self.sizes))
            out.append(self.fetch(piece, back))
        return out


def chunks(pieces, rows, axis=0):
    size = pieces[0].shape[axis]
    many = max(1, rows // size)
    groups = [pieces[i : i + many] for i in range(0, len(pieces), many)]
    if many == 1:
        return pieces
    return [jnp.concatenate(g, axis=axis) for g in groups]


def per_device(digits, centers, weights, batch_points, labels, nystrom_points, eigvecs, corrections):
    count = math.prod(digits.sizes)
    scale = (centers.shape[0] * count) ** (-0.5)
    batch = labels.shape[0] * count
    plane, line, pair = (0, 2), (1,), (3,)
    halves = digits.sizes[3]
    rows = batch // halves
    n_centers, features = centers.shape
    outs = weights.shape[1]
    padded = pl.cdiv(outs, 128) * 128
    q = eigvecs.shape[1]
    nys = nystrom_points.shape[0] * digits.sizes[0] * digits.sizes[2] * halves
    total = batch + nys

    pieces = digits.gather(batch_points, line)
    piece = join(pieces)
    pieces = digits.gather(piece, plane)
    batch_own = join(pieces)
    batch_half = digits.gather(batch_own, pair)

    points_own = digits.gather(nystrom_points, plane)
    vectors_own = digits.gather(eigvecs.T, plane)
    points_own = chunks(points_own, 256)
    vectors_own = chunks(vectors_own, 256, axis=1)
    points = [digits.gather(p, pair) for p in points_own]
    vectors = [digits.gather(v, pair) for v in vectors_own]
    points = [[p[h] for p in points] for h in range(halves)]
    vectors = [[v[h] for v in vectors] for h in range(halves)]

    weights_t = weights.T
    weights_low, centers_sq, factors = call(
        prep_body,
        [
            shape((padded, n_centers), jnp.bfloat16),
            shape((1, n_centers)),
            shape((q, 128)),
        ],
        weights_t,
        centers,
        corrections[None, :],
        flops=4 * n_centers * features,
    )

    ordered = [p for group in points for p in group]
    buffer = tile_call(ordered[0], centers, centers_sq, None, batch, total)

    values = [None] * halves
    buffer, k_first = tile_call(batch_half[0], centers, centers_sq, buffer, 0, total, kept=True)
    for h in range(1, halves):
        buffer, values[h] = tile_call(
            batch_half[h], centers, centers_sq, buffer, h * rows, total, weights=weights_low
        )
    values[0] = call(
        value_body, [shape((rows, padded))], k_first, weights_low, flops=2 * rows * n_centers * outs
    )
    for dims, after in ((pair, plane), (plane, line)):
        values = digits.scatter(values, dims)
        cuts = len(digits.steps(after))
        cut = shape((values[0].shape[0] // cuts, padded))
        values = call(functools.partial(sum_body, len(values)), [cut] * cuts, *values)
        values = [values] if cuts == 1 else list(values)
    values = digits.scatter(values, line)
    residual = call(
        functools.partial(residual_body, scale, len(values)),
        [shape((labels.shape[0], padded), jnp.bfloat16)],
        *values,
        labels,
    )
    pieces = digits.gather(residual, line)
    residual = join(pieces)
    pieces = digits.gather(residual, plane)
    residual = join(pieces)
    residual = digits.gather(residual, pair)

    start = batch
    for i, p in enumerate(ordered):
        if i:
            buffer = tile_call(p, centers, centers_sq, buffer, start, total)
        start += p.shape[0]
    pulling, stacks = None, []
    for h in range(halves):
        last = h == halves - 1
        n = sum(p.shape[0] for p in points[h])
        some = [*batch_half, *points[h], *vectors[h]]
        if h:
            some.append(pulling)
        pulling, stack = pl.pallas_call(
            functools.partial(pull_body, halves, len(points[h]), h > 0),
            out_shape=(
                shape((3 * q, batch), jnp.bfloat16) if last else shape((q, batch)),
                shape((6 * q, n), jnp.bfloat16),
            ),
            in_specs=[pl.BlockSpec(memory_space=pltpu.VMEM)] * len(some),
            out_specs=(pl.BlockSpec(memory_space=pltpu.VMEM),) * 2,
            scratch_shapes=[
                pltpu.VMEM((n, batch), jnp.bfloat16),
                pltpu.VMEM((3 * q, n), jnp.bfloat16),
            ],
            compiler_params=pltpu.CompilerParams(vmem_limit_bytes=16 * MIB),
            cost_estimate=pl.CostEstimate(
                flops=2 * n * batch * (features + 3 * q),
                bytes_accessed=8 * MIB,
                transcendentals=2 * n * batch,
            ),
            name="pull",
        )(*some)
        stacks.append(stack)

    vmem = pl.BlockSpec(memory_space=pltpu.VMEM)
    hbm = pl.BlockSpec(memory_space=pl.ANY)
    new_t = pl.pallas_call(
        functools.partial(update_body, RATE / batch, halves, len(stacks)),
        out_shape=shape((outs, n_centers)),
        in_specs=[vmem] * (halves + 2) + [hbm] * (len(stacks) + 2),
        out_specs=hbm,
        scratch_shapes=[
            pltpu.VMEM((6 * q, nys), jnp.bfloat16),
            pltpu.VMEM((total, n_centers), jnp.bfloat16),
            pltpu.VMEM((outs, n_centers), jnp.float32),
            pltpu.VMEM((6 * q, padded), jnp.bfloat16),
            pltpu.VMEM((padded, total), jnp.bfloat16),
            pltpu.SemaphoreType.DMA((len(stacks) + 2,)),
            pltpu.SemaphoreType.DMA((pl.cdiv(outs, 256),)),
        ],
        compiler_params=pltpu.CompilerParams(vmem_limit_bytes=30 * MIB),
        cost_estimate=pl.CostEstimate(
            flops=2 * outs * (6 * q * nys + total * n_centers),
            bytes_accessed=24 * MIB,
            transcendentals=0,
        ),
        name="update",
    )(*residual, pulling, factors, *stacks, buffer, weights_t)
    return new_t.T


def solution(mesh):
    digits = Digits(mesh)
    rows = P(AXES, None)
    shared = P(("narrow", "nys"), None)

    def step(*args):
        return per_device(digits, *args)

    return jax.shard_map(
        step,
        mesh=mesh,
        in_specs=(rows, rows, rows, rows, shared, shared, P()),
        out_specs=rows,
        check_vma=False,
    )
```

time: 261 us -> 120 us (0.46)
  waiting for transfers between devices: 132 us -> 52.1 us
  blocking collectives: 61.8 us -> 0 us
  matrix products: 37.9 us -> 0 us
  Pallas kernels: 0 us -> 34.5 us
  starting transfers between devices: 0.3 us -> 27.1 us
  between operations: 13.3 us -> 0.49 us
  other arithmetic: 8.02 us -> 0 us
    all_gather x3 -> x0, waiting for transfers between devices: 76.4 us -> none  [the longest x1 48.4 us: per_device(): lax.all_gather(batch_points, ('narrow', 'wide', 'nys'), axis=0, tiled=True)]
    psum x1 -> x0, blocking collectives: 61.8 us -> none  [per_device(): lax.psum(partial_value - placed, ('narrow', 'wide', 'nys'))]
    psum x1 -> x0, waiting for transfers between devices: 53.8 us -> none  [per_device(): projected = lax.psum(local_proj, ('narrow', 'nys'))]
    ppermute x0 -> x35, waiting for transfers between devices: none -> 52.1 us  [fetch(): return lax.ppermute(value, AXES, self.perm(offsets))]
    dot_general x8 -> x0, matrix products: 37.9 us -> none  [the longest x2 13.8 us: kernel_with(): lax.dot_general(left, right, (((1,), (1,)), ((), ())), preferred_element_...]
    pallas_call x0 -> x22, Pallas kernels: none -> 34.5 us  [the longest x1 13.7 us: per_device(): pl.pallas_call(functools.partial(update_body, RATE / batch, halves, len(s...]
    ppermute x0 -> x35, starting transfers between devices: none -> 27.1 us  [fetch(): return lax.ppermute(value, AXES, self.perm(offsets))]
    reduce_sum x4 -> x0, other arithmetic: 8.02 us -> none  [the longest x2 4.73 us: kernel_with(): right_sq = jnp.sum(jnp.square(right.astype(jnp.float32)), axis=1)]
  transfers between devices with their start and end apart: 4 -> 35, of which waited for: 3 -> 21; matrix products, arithmetic and copies ran while one was open for 12% -> 0% of each run, Pallas kernels for 0% -> 16%
where the time goes in v1:
time: 120 us; the launch traced here: 119 us
  waiting for transfers between devices  52.1 us (43%)
  Pallas kernels  34.5 us (29%)
  starting transfers between devices  27.1 us (23%)
  local copies, waits for them, and re-layouts  5.21 us (4%)
    ppermute x35, waiting for transfers between devices, fetch(): return lax.ppermute(value, AXES, self.perm(offsets))  52.1 us
    ppermute x35, starting transfers between devices, fetch(): return lax.ppermute(value, AXES, self.perm(offsets))  27.1 us
    pallas_call x1, Pallas kernels, per_device(): pl.pallas_call(functools.partial(update_body, RATE / batch, halves, len(s...  13.7 us
    pallas_call x10, Pallas kernels, tile_call(): pl.pallas_call(functools.partial(tile_body, start, kept, weights is not N...  13.6 us
    pallas_call x2, Pallas kernels, per_device(): pl.pallas_call(functools.partial(pull_body, halves, len(points[h]), h > 0...  5.33 us
    unnamed x18, local copies, waits for them, and re-layouts  5.21 us
  transfers between devices with their start and end apart: 35, of which 21 were waited for; matrix products, arithmetic and copies ran while one was open for 0% of the time, Pallas kernels for 16%

profile of v1, /device:TPU:0, one launch (start us, length us, event | category | flops | bytes accessed | tf_op | source)
XLA Modules:
  0.0 119.3 jit_solution(4134450705077199028)
XLA Ops:
  0.0 5.1 %collective-permute-start = (bf16[16,1024]{1,0:T(8,128)(2,1)}, bf16[16,1024]{1,0:T(8,128)(2,1)S(1)}, u32[]{:S(2)}, u32[]{:S(2)}) collective-permute-start(bf16[16,1024]{1,0:T(8,128)(2,1)} %refs_0_.2), channel_id=1, source_target_pairs={{4,0},{5,1},{6,2},{7,3},{8,4},{9,5},{10,6},{11,7},{12,8},{13,9},{1... | collective-permute-start | bytes 98312 | tf_op jit(solution)/shard_map/ppermute | solution.py:296
  7.0 3.1 %collective-permute-done.1.refs_2_ = bf16[16,1024]{1,0:T(8,128)(2,1)S(1)} collective-permute-done((bf16[16,1024]{1,0:T(8,128)(2,1)}, bf16[16,1024]{1,0:T(8,128)(2,1)S(1)}, u32[]{:S(2)}, u32[]{:S(2)}) %collective-permute-start.1) | collective-permute-done | bytes 32800 | tf_op jit(solution)/shard_map/ppermute | solution.py:296
  11.8 1.6 %collective-permute-start.3 = (bf16[64,1024]{1,0:T(8,128)(2,1)S(1)}, bf16[64,1024]{1,0:T(8,128)(2,1)S(1)}, u32[]{:S(2)}, u32[]{:S(2)}) collective-permute-start(bf16[64,1024]{1,0:T(8,128)(2,1)S(1)} %shard_map.73.refs_0_), channel_id=1, source_target_pairs={{2,0},{3,1},{0,2},{1,3},{6,4},{7,5},{4,6},{5,7},{10,8},{11,9},{8,1... | collective-permute-start | bytes 393224 | tf_op jit(solution)/shard_map/ppermute | solution.py:296
  13.3 1.5 %collective-permute-start.4 = (bf16[64,1024]{1,0:T(8,128)(2,1)S(1)}, bf16[64,1024]{1,0:T(8,128)(2,1)S(1)}, u32[]{:S(2)}, u32[]{:S(2)}) collective-permute-start(bf16[64,1024]{1,0:T(8,128)(2,1)S(1)} %shard_map.73.refs_0_), channel_id=1, source_target_pairs={{16,0},{17,1},{18,2},{19,3},{20,4},{21,5},{22,6},{23,7},{24,8},{25... | collective-permute-start | bytes 393224 | tf_op jit(solution)/shard_map/ppermute | solution.py:296
  15.3 2.7 %collective-permute-done.3.refs_1_ = bf16[64,1024]{1,0:T(8,128)(2,1)S(1)} collective-permute-done((bf16[64,1024]{1,0:T(8,128)(2,1)S(1)}, bf16[64,1024]{1,0:T(8,128)(2,1)S(1)}, u32[]{:S(2)}, u32[]{:S(2)}) %collective-permute-start.3) | collective-permute-done | bytes 131104 | tf_op jit(solution)/shard_map/ppermute | solution.py:296
  19.3 1.5 %collective-permute-done.5.refs_3_ = bf16[64,1024]{1,0:T(8,128)(2,1)S(1)} collective-permute-done((bf16[64,1024]{1,0:T(8,128)(2,1)S(1)}, bf16[64,1024]{1,0:T(8,128)(2,1)S(1)}, u32[]{:S(2)}, u32[]{:S(2)}) %collective-permute-start.5) | collective-permute-done | bytes 131104 | tf_op jit(solution)/shard_map/ppermute | solution.py:296
  20.9 1.6 %copy-done = bf16[1024,1024]{1,0:T(8,128)(2,1)S(1)} copy-done((bf16[1024,1024]{1,0:T(8,128)(2,1)S(1)}, bf16[1024,1024]{1,0:T(8,128)(2,1)}, u32[]{:S(2)}) %copy-start) | copy-done | bytes 2097176
  22.4 2.2 %copy-done.2 = f32[1024,1000]{0,1:T(8,128)S(1)} copy-done((f32[1024,1000]{0,1:T(8,128)S(1)}, f32[1024,1000]{0,1:T(8,128)}, u32[]{:S(2)}) %copy-start.2) | copy-done | bytes 4096024
  27.4 1.3 %tile.11 = (bf16[2560,1024]{1,0:T(8,128)(2,1)S(1)}, bf16[256,1024]{1,0:T(8,128)(2,1)S(1)}) custom-call(bf16[256,1024]{1,0:T(8,128)(2,1)S(1)} %shard_map.74.refs_0_, bf16[1024,1024]{1,0:T(8,128)(2,1)S(1)} %copy-done, f32[1,1024]{1,0:T(1,128)S(1)} %get-tuple-element.24.refs_2_, bf16[2560,1024]{1,0:T(8,128)(2,1)S(1)} %tile.10.refs_3_), custom_call_target="tpu_custom_call", output_to_operand_aliasing={{0}: (3, {})} | custom-call | flops 536870912 | bytes 4194304 | tf_op jit(solution)/shard_map/tile/pallas_call | solution.py:154
  28.7 2.0 %tile.12 = (bf16[2560,1024]{1,0:T(8,128)(2,1)S(1)}, f32[256,1024]{1,0:T(8,128)S(1)}) custom-call(bf16[256,1024]{1,0:T(8,128)(2,1)S(1)} %collective-permute-done.6.refs_0_.refs_1_, bf16[1024,1024]{1,0:T(8,128)(2,1)S(1)} %copy-done, f32[1,1024]{1,0:T(1,128)S(1)} %get-tuple-element.24.refs_2_, ...), custom_call_target="tpu_custom_call", output_to_operand_aliasing={{0}: (4, {})} | custom-call | flops 1073741824 | bytes 4194304 | tf_op jit(solution)/shard_map/tile/pallas_call | solution.py:154
  32.1 1.5 %collective-permute-done.7.refs_1_ = f32[256,1024]{1,0:T(8,128)S(1)} collective-permute-done((f32[256,1024]{1,0:T(8,128)S(1)}, f32[256,1024]{1,0:T(8,128)S(1)}, u32[]{:S(2)}, u32[]{:S(2)}) %collective-permute-start.7) | collective-permute-done | bytes 1048608 | tf_op jit(solution)/shard_map/ppermute | solution.py:296
  34.3 1.9 %collective-permute-start.8 = (f32[64,1024]{1,0:T(8,128)S(1)}, f32[64,1024]{1,0:T(8,128)S(1)}, u32[]{:S(2)}, u32[]{:S(2)}) collective-permute-start(f32[64,1024]{1,0:T(8,128)S(1)} %get-tuple-element.30), channel_id=1, source_target_pairs={{2,0},{3,1},{0,2},{1,3},{6,4},{7,5},{4,6},{5,7},{10,8},{11,9},{8,1... | collective-permute-start | bytes 786440 | tf_op jit(solution)/shard_map/ppermute | solution.py:296
  38.3 5.6 %collective-permute-done.10.refs_3_ = f32[64,1024]{1,0:T(8,128)S(1)} collective-permute-done((f32[64,1024]{1,0:T(8,128)S(1)}, f32[64,1024]{1,0:T(8,128)S(1)}, u32[]{:S(2)}, u32[]{:S(2)}) %collective-permute-start.10) | collective-permute-done | bytes 262176 | tf_op jit(solution)/shard_map/ppermute | solution.py:296
  44.4 4.6 %collective-permute-done.8.refs_1_ = f32[64,1024]{1,0:T(8,128)S(1)} collective-permute-done((f32[64,1024]{1,0:T(8,128)S(1)}, f32[64,1024]{1,0:T(8,128)S(1)}, u32[]{:S(2)}, u32[]{:S(2)}) %collective-permute-start.8) | collective-permute-done | bytes 262176 | tf_op jit(solution)/shard_map/ppermute | solution.py:296
  49.2 1.4 %collective-permute-start.12 = (f32[16,1024]{1,0:T(8,128)S(1)}, f32[16,1024]{1,0:T(8,128)S(1)}, u32[]{:S(2)}, u32[]{:S(2)}) collective-permute-start(f32[16,1024]{1,0:T(8,128)S(1)} %get-tuple-element.35), channel_id=1, source_target_pairs={{8,0},{9,1},{10,2},{11,3},{12,4},{13,5},{14,6},{15,7},{0,8},{1,9},... | collective-permute-start | bytes 196616 | tf_op jit(solution)/shard_map/ppermute | solution.py:296
  50.6 5.1 %collective-permute-done.11.refs_1_ = f32[16,1024]{1,0:T(8,128)S(1)} collective-permute-done((f32[16,1024]{1,0:T(8,128)S(1)}, f32[16,1024]{1,0:T(8,128)S(1)}, u32[]{:S(2)}, u32[]{:S(2)}) %collective-permute-start.11) | collective-permute-done | bytes 65568 | tf_op jit(solution)/shard_map/ppermute | solution.py:296
  55.6 1.9 %collective-permute-done.12.refs_2_ = f32[16,1024]{1,0:T(8,128)S(1)} collective-permute-done((f32[16,1024]{1,0:T(8,128)S(1)}, f32[16,1024]{1,0:T(8,128)S(1)}, u32[]{:S(2)}, u32[]{:S(2)}) %collective-permute-start.12) | collective-permute-done | bytes 65568 | tf_op jit(solution)/shard_map/ppermute | solution.py:296
  57.5 2.4 %collective-permute-done.13.refs_3_ = f32[16,1024]{1,0:T(8,128)S(1)} collective-permute-done((f32[16,1024]{1,0:T(8,128)S(1)}, f32[16,1024]{1,0:T(8,128)S(1)}, u32[]{:S(2)}, u32[]{:S(2)}) %collective-permute-start.13) | collective-permute-done | bytes 65568 | tf_op jit(solution)/shard_map/ppermute | solution.py:296
  59.9 1.9 %collective-permute-start.14 = (bf16[16,1024]{1,0:T(8,128)(2,1)S(1)}, bf16[16,1024]{1,0:T(8,128)(2,1)S(1)}, u32[]{:S(2)}, u32[]{:S(2)}) collective-permute-start(bf16[16,1024]{1,0:T(8,128)(2,1)S(1)} %shard_map.79.refs_0_), channel_id=1, source_target_pairs={{4,0},{5,1},{6,2},{7,3},{8,4},{9,5},{10,6},{11,7},{12,8},{13,9},{1... | collective-permute-start | bytes 98312 | tf_op jit(solution)/shard_map/ppermute | solution.py:296
  61.8 2.1 %collective-permute-done.14.refs_1_ = bf16[16,1024]{1,0:T(8,128)(2,1)S(1)} collective-permute-done((bf16[16,1024]{1,0:T(8,128)(2,1)S(1)}, bf16[16,1024]{1,0:T(8,128)(2,1)S(1)}, u32[]{:S(2)}, u32[]{:S(2)}) %collective-permute-start.14) | collective-permute-done | bytes 32800 | tf_op jit(solution)/shard_map/ppermute | solution.py:296
  64.1 2.5 %collective-permute-done.15.refs_2_ = bf16[16,1024]{1,0:T(8,128)(2,1)S(1)} collective-permute-done((bf16[16,1024]{1,0:T(8,128)(2,1)S(1)}, bf16[16,1024]{1,0:T(8,128)(2,1)S(1)}, u32[]{:S(2)}, u32[]{:S(2)}) %collective-permute-start.15) | collective-permute-done | bytes 32800 | tf_op jit(solution)/shard_map/ppermute | solution.py:296
  67.1 2.5 %collective-permute-done.16.refs_3_ = bf16[16,1024]{1,0:T(8,128)(2,1)S(1)} collective-permute-done((bf16[16,1024]{1,0:T(8,128)(2,1)S(1)}, bf16[16,1024]{1,0:T(8,128)(2,1)S(1)}, u32[]{:S(2)}, u32[]{:S(2)}) %collective-permute-start.16) | collective-permute-done | bytes 32800 | tf_op jit(solution)/shard_map/ppermute | solution.py:296
  70.6 3.9 %collective-permute-done.29.refs_7_ = f32[160,256]{1,0:T(8,128)S(1)} collective-permute-done((f32[160,256]{1,0:T(8,128)S(1)}, f32[160,256]{1,0:T(8,128)S(1)}, u32[]{:S(2)}, u32[]{:S(2)}) %collective-permute-start.29) | collective-permute-done | bytes 163872 | tf_op jit(solution)/shard_map/ppermute | solution.py:296
  76.7 2.8 %collective-permute-done.17.refs_1_ = bf16[64,1024]{1,0:T(8,128)(2,1)S(1)} collective-permute-done((bf16[64,1024]{1,0:T(8,128)(2,1)S(1)}, bf16[64,1024]{1,0:T(8,128)(2,1)S(1)}, u32[]{:S(2)}, u32[]{:S(2)}) %collective-permute-start.17) | collective-permute-done | bytes 131104 | tf_op jit(solution)/shard_map/ppermute | solution.py:296
  79.9 2.1 %collective-permute-start.19 = (bf16[64,1024]{1,0:T(8,128)(2,1)S(1)}, bf16[64,1024]{1,0:T(8,128)(2,1)S(1)}, u32[]{:S(2)}, u32[]{:S(2)}) collective-permute-start(bf16[64,1024]{1,0:T(8,128)(2,1)S(1)} %shard_map.80.refs_0_), channel_id=1, source_target_pairs={{18,0},{19,1},{16,2},{17,3},{22,4},{23,5},{20,6},{21,7},{26,8},{27... | collective-permute-start | bytes 393224 | tf_op jit(solution)/shard_map/ppermute | solution.py:296
  82.0 4.3 %collective-permute-done.19.refs_3_ = bf16[64,1024]{1,0:T(8,128)(2,1)S(1)} collective-permute-done((bf16[64,1024]{1,0:T(8,128)(2,1)S(1)}, bf16[64,1024]{1,0:T(8,128)(2,1)S(1)}, u32[]{:S(2)}, u32[]{:S(2)}) %collective-permute-start.19) | collective-permute-done | bytes 131104 | tf_op jit(solution)/shard_map/ppermute | solution.py:296
  86.2 1.6 %collective-permute-start.33 = (f32[160,256]{1,0:T(8,128)S(1)}, f32[160,256]{1,0:T(8,128)S(1)}, u32[]{:S(2)}, u32[]{:S(2)}) collective-permute-start(f32[160,256]{1,0:T(8,128)S(1)} %bitcast.9), channel_id=1, source_target_pairs={{18,0},{19,1},{16,2},{17,3},{22,4},{23,5},{20,6},{21,7},{26,8},{27... | collective-permute-start | bytes 491528 | tf_op jit(solution)/shard_map/ppermute | solution.py:296
  87.8 1.4 %tile.13.refs_3_ = bf16[2560,1024]{1,0:T(8,128)(2,1)S(1)} custom-call(bf16[256,1024]{1,0:T(8,128)(2,1)S(1)} %collective-permute-done.22.refs_3_.refs_0_, bf16[1024,1024]{1,0:T(8,128)(2,1)S(1)} %copy-done, f32[1,1024]{1,0:T(1,128)S(1)} %get-tuple-element.24.refs_2_, bf16[2560,1024]{1,0:T(8,128)(2,1)S(1)} %get-tuple-element.42.refs_3_), custom_call_target="tpu_custom_call", output_to_operand_aliasing={{}: (3, {})} | custom-call | flops 536870912 | bytes 4194304 | tf_op jit(solution)/shard_map/tile/pallas_call | solution.py:154
  90.6 1.9 %collective-permute-done.33.refs_9_ = f32[160,256]{1,0:T(8,128)S(1)} collective-permute-done((f32[160,256]{1,0:T(8,128)S(1)}, f32[160,256]{1,0:T(8,128)S(1)}, u32[]{:S(2)}, u32[]{:S(2)}) %collective-permute-start.33) | collective-permute-done | bytes 163872 | tf_op jit(solution)/shard_map/ppermute | solution.py:296
  93.8 2.7 %pull.2 = (f32[160,512]{1,0:T(8,128)S(1)}, bf16[960,1024]{1,0:T(8,128)(2,1)S(1)}) custom-call(bf16[256,1024]{1,0:T(8,128)(2,1)S(1)} %shard_map.74.refs_0_, bf16[256,1024]{1,0:T(8,128)(2,1)S(1)} %collective-permute-done.6.refs_0_.refs_1_, bf16[256,1024]{1,0:T(8,128)(2,1)S(1)} %copy-done.4, bf16[256,1024]{1,0:T(8,128)(2,1)S(1)} %collective-permute-done.22.refs_3_.refs_0_, ...), custom_call_target="tpu_custom_call" | custom-call | flops 1577058304 | bytes 8388608 | tf_op jit(solution)/shard_map/pull/pallas_call | solution.py:404
  102.7 2.7 %pull.3 = (bf16[480,512]{1,0:T(8,128)(2,1)S(1)}, bf16[960,1024]{1,0:T(8,128)(2,1)S(1)}) custom-call(bf16[256,1024]{1,0:T(8,128)(2,1)S(1)} %shard_map.74.refs_0_, bf16[256,1024]{1,0:T(8,128)(2,1)S(1)} %collective-permute-done.6.refs_0_.refs_1_, bf16[256,1024]{1,0:T(8,128)(2,1)S(1)} %collective-permute-done.21.refs_2_.refs_0_, ...), custom_call_target="tpu_custom_call" | custom-call | flops 1577058304 | bytes 8388608 | tf_op jit(solution)/shard_map/pull/pallas_call | solution.py:404
  105.4 13.7 %update.1 = f32[1000,1024]{1,0:T(8,128)} custom-call(bf16[256,1024]{1,0:T(8,128)(2,1)S(1)} %shard_map.81.refs_0_, bf16[256,1024]{1,0:T(8,128)(2,1)S(1)} %collective-permute-done.20.refs_1_, bf16[480,512]{1,0:T(8,128)(2,1)S(1)} %get-tuple-element.38.refs_2_, f32[160,128]{1,0:T(8,128)S(1)} %get-tuple-element.39.refs_3_, ...), custom_call_target="tpu_custom_call" | custom-call | flops 9175040000 | bytes 25165824 | tf_op jit(solution)/shard_map/update/pallas_call | solution.py:428
  (78 shorter events, 26.1 us)
Async XLA Ops:
  0.0 7.0 %collective-permute-start = (bf16[16,1024]{1,0:T(8,128)(2,1)}, bf16[16,1024]{1,0:T(8,128)(2,1)S(1)}, u32[]{:S(2)}, u32[]{:S(2)}) collective-permute-start(bf16[16,1024]{1,0:T(8,128)(2,1)} %refs_0_.2), channel_id=1, source_target_pairs={{4,0},{5,1},{6,2},{7,3},{8,4},{9,5},{10,6},{11,7},{12,8},{13,9},{1... | collective-permute-start | bytes 98312 | tf_op jit(solution)/shard_map/ppermute | solution.py:296
  5.1 5.0 %collective-permute-start.1 = (bf16[16,1024]{1,0:T(8,128)(2,1)}, bf16[16,1024]{1,0:T(8,128)(2,1)S(1)}, u32[]{:S(2)}, u32[]{:S(2)}) collective-permute-start(bf16[16,1024]{1,0:T(8,128)(2,1)} %refs_0_.2), channel_id=1, source_target_pairs={{8,0},{9,1},{10,2},{11,3},{12,4},{13,5},{14,6},{15,7},{0,8},{1,9},... | collective-permute-start | bytes 98312 | tf_op jit(solution)/shard_map/ppermute | solution.py:296
  5.1 5.9 %collective-permute-start.2 = (bf16[16,1024]{1,0:T(8,128)(2,1)}, bf16[16,1024]{1,0:T(8,128)(2,1)S(1)}, u32[]{:S(2)}, u32[]{:S(2)}) collective-permute-start(bf16[16,1024]{1,0:T(8,128)(2,1)} %refs_0_.2), channel_id=1, source_target_pairs={{12,0},{13,1},{14,2},{15,3},{0,4},{1,5},{2,6},{3,7},{4,8},{5,9},{6... | collective-permute-start | bytes 98312 | tf_op jit(solution)/shard_map/ppermute | solution.py:296
  11.8 6.3 %collective-permute-start.3 = (bf16[64,1024]{1,0:T(8,128)(2,1)S(1)}, bf16[64,1024]{1,0:T(8,128)(2,1)S(1)}, u32[]{:S(2)}, u32[]{:S(2)}) collective-permute-start(bf16[64,1024]{1,0:T(8,128)(2,1)S(1)} %shard_map.73.refs_0_), channel_id=1, source_target_pairs={{2,0},{3,1},{0,2},{1,3},{6,4},{7,5},{4,6},{5,7},{10,8},{11,9},{8,1... | collective-permute-start | bytes 393224 | tf_op jit(solution)/shard_map/ppermute | solution.py:296
  13.3 5.9 %collective-permute-start.4 = (bf16[64,1024]{1,0:T(8,128)(2,1)S(1)}, bf16[64,1024]{1,0:T(8,128)(2,1)S(1)}, u32[]{:S(2)}, u32[]{:S(2)}) collective-permute-start(bf16[64,1024]{1,0:T(8,128)(2,1)S(1)} %shard_map.73.refs_0_), channel_id=1, source_target_pairs={{16,0},{17,1},{18,2},{19,3},{20,4},{21,5},{22,6},{23,7},{24,8},{25... | collective-permute-start | bytes 393224 | tf_op jit(solution)/shard_map/ppermute | solution.py:296
  14.9 5.9 %collective-permute-start.5 = (bf16[64,1024]{1,0:T(8,128)(2,1)S(1)}, bf16[64,1024]{1,0:T(8,128)(2,1)S(1)}, u32[]{:S(2)}, u32[]{:S(2)}) collective-permute-start(bf16[64,1024]{1,0:T(8,128)(2,1)S(1)} %shard_map.73.refs_0_), channel_id=1, source_target_pairs={{18,0},{19,1},{16,2},{17,3},{22,4},{23,5},{20,6},{21,7},{26,8},{27... | collective-permute-start | bytes 393224 | tf_op jit(solution)/shard_map/ppermute | solution.py:296
  20.8 7.9 %collective-permute-start.6 = (bf16[256,1024]{1,0:T(8,128)(2,1)S(1)}, bf16[256,1024]{1,0:T(8,128)(2,1)S(1)}, u32[]{:S(2)}, u32[]{:S(2)}) collective-permute-start(bf16[256,1024]{1,0:T(8,128)(2,1)S(1)} %shard_map.74.refs_0_), channel_id=1, source_target_pairs={{1,0},{0,1},{3,2},{2,3},{5,4},{4,5},{7,6},{6,7},{9,8},{8,9},{11,10... | collective-permute-start | bytes 1572872 | tf_op jit(solution)/shard_map/ppermute | solution.py:296
  33.7 10.2 %collective-permute-start.10 = (f32[64,1024]{1,0:T(8,128)S(1)}, f32[64,1024]{1,0:T(8,128)S(1)}, u32[]{:S(2)}, u32[]{:S(2)}) collective-permute-start(f32[64,1024]{1,0:T(8,128)S(1)} %get-tuple-element.32), channel_id=1, source_target_pairs={{18,0},{19,1},{16,2},{17,3},{22,4},{23,5},{20,6},{21,7},{26,8},{27... | collective-permute-start | bytes 786440 | tf_op jit(solution)/shard_map/ppermute | solution.py:296
  34.3 14.7 %collective-permute-start.8 = (f32[64,1024]{1,0:T(8,128)S(1)}, f32[64,1024]{1,0:T(8,128)S(1)}, u32[]{:S(2)}, u32[]{:S(2)}) collective-permute-start(f32[64,1024]{1,0:T(8,128)S(1)} %get-tuple-element.30), channel_id=1, source_target_pairs={{2,0},{3,1},{0,2},{1,3},{6,4},{7,5},{4,6},{5,7},{10,8},{11,9},{8,1... | collective-permute-start | bytes 786440 | tf_op jit(solution)/shard_map/ppermute | solution.py:296
  36.2 12.8 %collective-permute-start.9 = (f32[64,1024]{1,0:T(8,128)S(1)}, f32[64,1024]{1,0:T(8,128)S(1)}, u32[]{:S(2)}, u32[]{:S(2)}) collective-permute-start(f32[64,1024]{1,0:T(8,128)S(1)} %get-tuple-element.31), channel_id=1, source_target_pairs={{16,0},{17,1},{18,2},{19,3},{20,4},{21,5},{22,6},{23,7},{24,8},{25... | collective-permute-start | bytes 786440 | tf_op jit(solution)/shard_map/ppermute | solution.py:296
  37.3 38.8 %collective-permute-start.22 = (bf16[256,1024]{1,0:T(8,128)(2,1)S(1)}, bf16[256,1024]{1,0:T(8,128)(2,1)S(1)}, u32[]{:S(2)}, u32[]{:S(2)}) collective-permute-start(bf16[256,1024]{1,0:T(8,128)(2,1)S(1)} %copy-done.4), channel_id=1, source_target_pairs={{2,0},{3,1},{0,2},{1,3},{6,4},{7,5},{4,6},{5,7},{10,8},{11,9},{8,1... | collective-permute-start | bytes 1572872 | tf_op jit(solution)/shard_map/ppermute | solution.py:296
  37.8 38.3 %collective-permute-start.24 = (bf16[256,1024]{1,0:T(8,128)(2,1)S(1)}, bf16[256,1024]{1,0:T(8,128)(2,1)S(1)}, u32[]{:S(2)}, u32[]{:S(2)}) collective-permute-start(bf16[256,1024]{1,0:T(8,128)(2,1)S(1)} %copy-done.4), channel_id=1, source_target_pairs={{16,0},{17,1},{18,2},{19,3},{20,4},{21,5},{22,6},{23,7},{24,8},{25... | collective-permute-start | bytes 1572872 | tf_op jit(solution)/shard_map/ppermute | solution.py:296
  43.9 32.7 %collective-permute-start.26 = (bf16[256,1024]{1,0:T(8,128)(2,1)S(1)}, bf16[256,1024]{1,0:T(8,128)(2,1)S(1)}, u32[]{:S(2)}, u32[]{:S(2)}) collective-permute-start(bf16[256,1024]{1,0:T(8,128)(2,1)S(1)} %copy-done.4), channel_id=1, source_target_pairs={{18,0},{19,1},{16,2},{17,3},{22,4},{23,5},{20,6},{21,7},{26,8},{27... | collective-permute-start | bytes 1572872 | tf_op jit(solution)/shard_map/ppermute | solution.py:296
  49.1 6.5 %collective-permute-start.11 = (f32[16,1024]{1,0:T(8,128)S(1)}, f32[16,1024]{1,0:T(8,128)S(1)}, u32[]{:S(2)}, u32[]{:S(2)}) collective-permute-start(f32[16,1024]{1,0:T(8,128)S(1)} %get-tuple-element.34), channel_id=1, source_target_pairs={{12,0},{13,1},{14,2},{15,3},{0,4},{1,5},{2,6},{3,7},{4,8},{5,9},{6... | collective-permute-start | bytes 196616 | tf_op jit(solution)/shard_map/ppermute | solution.py:296
  49.2 8.4 %collective-permute-start.12 = (f32[16,1024]{1,0:T(8,128)S(1)}, f32[16,1024]{1,0:T(8,128)S(1)}, u32[]{:S(2)}, u32[]{:S(2)}) collective-permute-start(f32[16,1024]{1,0:T(8,128)S(1)} %get-tuple-element.35), channel_id=1, source_target_pairs={{8,0},{9,1},{10,2},{11,3},{12,4},{13,5},{14,6},{15,7},{0,8},{1,9},... | collective-permute-start | bytes 196616 | tf_op jit(solution)/shard_map/ppermute | solution.py:296
  61.8 4.8 %collective-permute-start.15 = (bf16[16,1024]{1,0:T(8,128)(2,1)S(1)}, bf16[16,1024]{1,0:T(8,128)(2,1)S(1)}, u32[]{:S(2)}, u32[]{:S(2)}) collective-permute-start(bf16[16,1024]{1,0:T(8,128)(2,1)S(1)} %shard_map.79.refs_0_), channel_id=1, source_target_pairs={{8,0},{9,1},{10,2},{11,3},{12,4},{13,5},{14,6},{15,7},{0,8},{1,9},... | collective-permute-start | bytes 98312 | tf_op jit(solution)/shard_map/ppermute | solution.py:296
  63.9 5.7 %collective-permute-start.16 = (bf16[16,1024]{1,0:T(8,128)(2,1)S(1)}, bf16[16,1024]{1,0:T(8,128)(2,1)S(1)}, u32[]{:S(2)}, u32[]{:S(2)}) collective-permute-start(bf16[16,1024]{1,0:T(8,128)(2,1)S(1)} %shard_map.79.refs_0_), channel_id=1, source_target_pairs={{12,0},{13,1},{14,2},{15,3},{0,4},{1,5},{2,6},{3,7},{4,8},{5,9},{6... | collective-permute-start | bytes 98312 | tf_op jit(solution)/shard_map/ppermute | solution.py:296
  66.6 7.9 %collective-permute-start.29 = (f32[160,256]{1,0:T(8,128)S(1)}, f32[160,256]{1,0:T(8,128)S(1)}, u32[]{:S(2)}, u32[]{:S(2)}) collective-permute-start(f32[160,256]{1,0:T(8,128)S(1)} %bitcast.7), channel_id=1, source_target_pairs={{2,0},{3,1},{0,2},{1,3},{6,4},{7,5},{4,6},{5,7},{10,8},{11,9},{8,1... | collective-permute-start | bytes 491528 | tf_op jit(solution)/shard_map/ppermute | solution.py:296
  69.6 5.3 %collective-permute-start.31 = (f32[160,256]{1,0:T(8,128)S(1)}, f32[160,256]{1,0:T(8,128)S(1)}, u32[]{:S(2)}, u32[]{:S(2)}) collective-permute-start(f32[160,256]{1,0:T(8,128)S(1)} %bitcast.8), channel_id=1, source_target_pairs={{16,0},{17,1},{18,2},{19,3},{20,4},{21,5},{22,6},{23,7},{24,8},{25... | collective-permute-start | bytes 491528 | tf_op jit(solution)/shard_map/ppermute | solution.py:296
  74.5 5.0 %collective-permute-start.17 = (bf16[64,1024]{1,0:T(8,128)(2,1)S(1)}, bf16[64,1024]{1,0:T(8,128)(2,1)S(1)}, u32[]{:S(2)}, u32[]{:S(2)}) collective-permute-start(bf16[64,1024]{1,0:T(8,128)(2,1)S(1)} %shard_map.80.refs_0_), channel_id=1, source_target_pairs={{2,0},{3,1},{0,2},{1,3},{6,4},{7,5},{4,6},{5,7},{10,8},{11,9},{8,1... | collective-permute-start | bytes 393224 | tf_op jit(solution)/shard_map/ppermute | solution.py:296
  74.9 5.0 %collective-permute-start.18 = (bf16[64,1024]{1,0:T(8,128)(2,1)S(1)}, bf16[64,1024]{1,0:T(8,128)(2,1)S(1)}, u32[]{:S(2)}, u32[]{:S(2)}) collective-permute-start(bf16[64,1024]{1,0:T(8,128)(2,1)S(1)} %shard_map.80.refs_0_), channel_id=1, source_target_pairs={{16,0},{17,1},{18,2},{19,3},{20,4},{21,5},{22,6},{23,7},{24,8},{25... | collective-permute-start | bytes 393224 | tf_op jit(solution)/shard_map/ppermute | solution.py:296
  76.1 20.4 %collective-permute-start.21 = (bf16[256,1024]{1,0:T(8,128)(2,1)S(1)}, bf16[256,1024]{1,0:T(8,128)(2,1)S(1)}, u32[]{:S(2)}, u32[]{:S(2)}) collective-permute-start(bf16[256,1024]{1,0:T(8,128)(2,1)S(1)} %copy-done.4), channel_id=1, source_target_pairs={{1,0},{0,1},{3,2},{2,3},{5,4},{4,5},{7,6},{6,7},{9,8},{8,9},{11,10... | collective-permute-start | bytes 1572872 | tf_op jit(solution)/shard_map/ppermute | solution.py:296
  76.1 20.9 %collective-permute-start.23 = (bf16[256,1024]{1,0:T(8,128)(2,1)S(1)}, bf16[256,1024]{1,0:T(8,128)(2,1)S(1)}, u32[]{:S(2)}, u32[]{:S(2)}) collective-permute-start(bf16[256,1024]{1,0:T(8,128)(2,1)S(1)} %collective-permute-done.22.refs_3_.refs_0_), channel_id=1, source_target_pairs={{1,0},{0,1},{3,2},{2,3},{5,4},{4,5},{7,6},{6,7},{9,8},{8,9},{11,10... | collective-permute-start | bytes 1572872 | tf_op jit(solution)/shard_map/ppermute | solution.py:296
  76.6 20.5 %collective-permute-start.25 = (bf16[256,1024]{1,0:T(8,128)(2,1)S(1)}, bf16[256,1024]{1,0:T(8,128)(2,1)S(1)}, u32[]{:S(2)}, u32[]{:S(2)}) collective-permute-start(bf16[256,1024]{1,0:T(8,128)(2,1)S(1)} %collective-permute-done.24.refs_4_.refs_0_), channel_id=1, source_target_pairs={{1,0},{0,1},{3,2},{2,3},{5,4},{4,5},{7,6},{6,7},{9,8},{8,9},{11,10... | collective-permute-start | bytes 1572872 | tf_op jit(solution)/shard_map/ppermute | solution.py:296
  79.4 18.1 %collective-permute-start.27 = (bf16[256,1024]{1,0:T(8,128)(2,1)S(1)}, bf16[256,1024]{1,0:T(8,128)(2,1)S(1)}, u32[]{:S(2)}, u32[]{:S(2)}) collective-permute-start(bf16[256,1024]{1,0:T(8,128)(2,1)S(1)} %collective-permute-done.26.refs_5_.refs_0_), channel_id=1, source_target_pairs={{1,0},{0,1},{3,2},{2,3},{5,4},{4,5},{7,6},{6,7},{9,8},{8,9},{11,10... | collective-permute-start | bytes 1572872 | tf_op jit(solution)/shard_map/ppermute | solution.py:296
  79.9 6.4 %collective-permute-start.19 = (bf16[64,1024]{1,0:T(8,128)(2,1)S(1)}, bf16[64,1024]{1,0:T(8,128)(2,1)S(1)}, u32[]{:S(2)}, u32[]{:S(2)}) collective-permute-start(bf16[64,1024]{1,0:T(8,128)(2,1)S(1)} %shard_map.80.refs_0_), channel_id=1, source_target_pairs={{18,0},{19,1},{16,2},{17,3},{22,4},{23,5},{20,6},{21,7},{26,8},{27... | collective-permute-start | bytes 393224 | tf_op jit(solution)/shard_map/ppermute | solution.py:296
  86.2 6.2 %collective-permute-start.33 = (f32[160,256]{1,0:T(8,128)S(1)}, f32[160,256]{1,0:T(8,128)S(1)}, u32[]{:S(2)}, u32[]{:S(2)}) collective-permute-start(f32[160,256]{1,0:T(8,128)S(1)} %bitcast.9), channel_id=1, source_target_pairs={{18,0},{19,1},{16,2},{17,3},{22,4},{23,5},{20,6},{21,7},{26,8},{27... | collective-permute-start | bytes 491528 | tf_op jit(solution)/shard_map/ppermute | solution.py:296
  92.5 12.9 %collective-permute-start.20 = (bf16[256,1024]{1,0:T(8,128)(2,1)S(1)}, bf16[256,1024]{1,0:T(8,128)(2,1)S(1)}, u32[]{:S(2)}, u32[]{:S(2)}) collective-permute-start(bf16[256,1024]{1,0:T(8,128)(2,1)S(1)} %shard_map.81.refs_0_), channel_id=1, source_target_pairs={{1,0},{0,1},{3,2},{2,3},{5,4},{4,5},{7,6},{6,7},{9,8},{8,9},{11,10... | collective-permute-start | bytes 1572872 | tf_op jit(solution)/shard_map/ppermute | solution.py:296
  96.4 6.3 %collective-permute-start.28 = (f32[160,256]{1,0:T(8,128)S(1)}, f32[160,256]{1,0:T(8,128)S(1)}, u32[]{:S(2)}, u32[]{:S(2)}) collective-permute-start(f32[160,256]{1,0:T(8,128)S(1)} %bitcast.11), channel_id=1, source_target_pairs={{1,0},{0,1},{3,2},{2,3},{5,4},{4,5},{7,6},{6,7},{9,8},{8,9},{11,10... | collective-permute-start | bytes 491528 | tf_op jit(solution)/shard_map/ppermute | solution.py:296
  97.0 5.7 %collective-permute-start.30 = (f32[160,256]{1,0:T(8,128)S(1)}, f32[160,256]{1,0:T(8,128)S(1)}, u32[]{:S(2)}, u32[]{:S(2)}) collective-permute-start(f32[160,256]{1,0:T(8,128)S(1)} %collective-permute-done.29.refs_7_), channel_id=1, source_target_pairs={{1,0},{0,1},{3,2},{2,3},{5,4},{4,5},{7,6},{6,7},{9,8},{8,9},{11,10... | collective-permute-start | bytes 491528 | tf_op jit(solution)/shard_map/ppermute | solution.py:296
  97.1 5.6 %collective-permute-start.32 = (f32[160,256]{1,0:T(8,128)S(1)}, f32[160,256]{1,0:T(8,128)S(1)}, u32[]{:S(2)}, u32[]{:S(2)}) collective-permute-start(f32[160,256]{1,0:T(8,128)S(1)} %collective-permute-done.31.refs_8_), channel_id=1, source_target_pairs={{1,0},{0,1},{3,2},{2,3},{5,4},{4,5},{7,6},{6,7},{9,8},{8,9},{11,10... | collective-permute-start | bytes 491528 | tf_op jit(solution)/shard_map/ppermute | solution.py:296
  97.5 5.2 %collective-permute-start.34 = (f32[160,256]{1,0:T(8,128)S(1)}, f32[160,256]{1,0:T(8,128)S(1)}, u32[]{:S(2)}, u32[]{:S(2)}) collective-permute-start(f32[160,256]{1,0:T(8,128)S(1)} %collective-permute-done.33.refs_9_), channel_id=1, source_target_pairs={{1,0},{0,1},{3,2},{2,3},{5,4},{4,5},{7,6},{6,7},{9,8},{8,9},{11,10... | collective-permute-start | bytes 491528 | tf_op jit(solution)/shard_map/ppermute | solution.py:296
  (12 other events, 114.0 us)
